TPU v7x, 32 devices: a whole 2x2x4 slice. The times are simulated.
32 devices in a mesh: shot: 2 (over x), freq: 16 (over z, y, core).
Axes of the slice: x: 2, y: 2, z: 4, core: 2. Of those that a mesh axis runs over, the one named last changes fastest.
Arguments:
- receiver_data: float32 [64, 2, 32, 1024], P(('shot', 'freq')), parts along dimension 0, may hold values from -6 to 6
- source_spectrum: float32 [32, 2], P('freq'), may hold values from -4 to 4
- filter_taps: float32 [32, 4, 6], P('freq'), may hold values from -1.5 to 1.5, as said below
- slowness: float32 [16, 32, 1024], P('freq'), may hold values from 0.5 to 2
- depth_owner: int32 [6], P('shot'), parts along dimension 0, may hold values from 0 to 15
- source_position: int32 [4], P('shot'), parts along dimension 0, may hold values from 0 to 31
Outputs:
- migrated_image: float32 [32, 32, 1024], P(('shot', 'freq')), parts along dimension 0
There are 2 independent parts, one for each index of `shot`. A program takes and returns all parts, laid end to end along the dimension named above; an argument that names none is the same for every part. Nothing has to cross between parts.
Inputs may be any that keep to these rules, and one draw needn't show every extreme that they name: `filter_taps`: each frequency and direction holds three complex taps.
All inputs are finite; a program needn't handle non-finite values.
Results may differ from a plain program's by a relative error of at most 0.0001.
Values sent between devices are 32-bit elements; how exact they have to be, the bound alone decides.
A program may use at most 64 MiB of HBM per device.

v0:
```python
import math
import jax
import jax.numpy as jnp
from jax import lax
from jax.sharding import PartitionSpec as P

lens_rate = 3.0
wave_rate = 0.5
directions = ((1, 0), (0, 1), (1, 1), (1, -1))


def broadcast(value, axis, source):
    kept = jnp.where(lax.axis_index(axis) == source, value, 0).astype(value.dtype)
    return lax.psum(kept, axis)


def source_start(spectrum, position, freq_index, freq_total, height, breadth):
    src_row = position[0].astype(jnp.float32)
    src_col = position[1].astype(jnp.float32)
    row_axis = jnp.arange(height, dtype=jnp.float32)[:, None]
    col_axis = jnp.arange(breadth, dtype=jnp.float32)[None, :]
    distance = jnp.sqrt((row_axis - src_row) ** 2 + (col_axis - src_col) ** 2 + 1.0)
    amplitude = 1.0 / (1.0 + distance / (height / 4.0))
    wavenumber = (freq_index.astype(jnp.float32) + 1.0) * (wave_rate / freq_total)
    phase_map = wavenumber[:, None, None] * distance[None]
    base_re = amplitude[None] * jnp.cos(phase_map)
    base_im = -amplitude[None] * jnp.sin(phase_map)
    wave_re = spectrum[:, 0][:, None, None]
    wave_im = spectrum[:, 1][:, None, None]
    return jnp.stack(
        [wave_re * base_re - wave_im * base_im, wave_re * base_im + wave_im * base_re], axis=1
    )


def complex_mul(values, coef_re, coef_im):
    coef_re = coef_re[:, None, None]
    coef_im = coef_im[:, None, None]
    return jnp.stack(
        [
            values[:, 0] * coef_re - values[:, 1] * coef_im,
            values[:, 0] * coef_im + values[:, 1] * coef_re,
        ],
        axis=1,
    )


def thin_lens(wavefield, layer_slab, freq_index, freq_total, handed):
    phases = (
        (freq_index.astype(jnp.float32) + 1.0)[:, None, None]
        * (lens_rate / freq_total)
        * layer_slab[None]
    )
    rot_re = jnp.cos(phases)
    rot_im = handed * jnp.sin(phases)
    part_re = wavefield[:, 0]
    part_im = wavefield[:, 1]
    return jnp.stack(
        [part_re * rot_re - part_im * rot_im, part_re * rot_im + part_im * rot_re], axis=1
    )


def directional(wavefield, coeffs, step_x, step_y, handed):
    height = wavefield.shape[2]
    breadth = wavefield.shape[3]
    padded = jnp.pad(wavefield, ((0, 0), (0, 0), (2, 2), (2, 2)))

    def adjacent(offset):
        return padded[
            :,
            :,
            2 + offset * step_x : 2 + offset * step_x + height,
            2 + offset * step_y : 2 + offset * step_y + breadth,
        ]

    inner_pair = adjacent(1) + adjacent(-1)
    outer_pair = adjacent(2) + adjacent(-2)
    result = complex_mul(wavefield, coeffs[:, 0], handed * coeffs[:, 1])
    result = result + complex_mul(inner_pair, coeffs[:, 2], handed * coeffs[:, 3])
    return result + complex_mul(outer_pair, coeffs[:, 4], handed * coeffs[:, 5])


def depth_step(source, receiver, layer_slab, filter_taps, freq_index, freq_total):
    source = thin_lens(source, layer_slab, freq_index, freq_total, -1.0)
    receiver = thin_lens(receiver, layer_slab, freq_index, freq_total, 1.0)
    for direction, (step_x, step_y) in enumerate(directions):
        source = directional(source, filter_taps[:, direction], step_x, step_y, 1.0)
        receiver = directional(receiver, filter_taps[:, direction], step_x, step_y, -1.0)
    return (source, receiver)


def local(receiver_data, source_spectrum, filter_taps, slowness, depth_owner, source_position):
    freq_local = receiver_data.shape[0]
    height = receiver_data.shape[2]
    breadth = receiver_data.shape[3]
    device_rank = lax.axis_index("freq")
    freq_total = lax.axis_size("freq") * freq_local
    freq_index = device_rank * freq_local + jnp.arange(freq_local, dtype=jnp.int32)
    source = source_start(source_spectrum, source_position, freq_index, freq_total, height, breadth)
    receiver = receiver_data
    migrated = jnp.zeros((1, height, breadth), jnp.float32)
    partials = []
    masks = []
    for level in range(depth_owner.shape[0]):
        owner_now = depth_owner[level]
        layer_slab = broadcast(slowness[0], "freq", owner_now)
        source, receiver = depth_step(
            source, receiver, layer_slab, filter_taps, freq_index, freq_total
        )
        local_term = jnp.sum(
            source[:, 0] * receiver[:, 0] + source[:, 1] * receiver[:, 1], axis=0
        ) / math.sqrt(freq_total)
        owner_mask = (owner_now == device_rank).astype(jnp.float32)
        partials.append(local_term)
        masks.append(owner_mask)
    summed_stack = lax.psum(jnp.stack(partials), "freq")
    for level in range(len(masks)):
        migrated = migrated + masks[level] * summed_stack[level][None]
    return migrated


def solution(mesh):
    return jax.shard_map(
        local,
        mesh=mesh,
        in_specs=(
            P(("shot", "freq"), None, None, None),
            P("freq", None),
            P("freq", None, None),
            P("freq", None, None),
            P("shot"),
            P("shot"),
        ),
        out_specs=P(("shot", "freq"), None, None),
        check_vma=False,
    )
```

profile of v0, /device:TPU:0, one launch (start us, length us, event | category | flops | bytes accessed | tf_op | source)
XLA Modules:
  0.0 240.8 jit_solution(6213239613544791227)
XLA Ops:
  6.5 0.7 copy-done.3
  7.2 0.6 fusion.131
  9.7 1.7 select_bitcast_fusion
  11.8 0.6 fusion.130
  14.9 91.4 %all-reduce.30.cloned.1.call-done = (f32[32,1024]{1,0:T(8,128)}, f32[32,1024]{1,0:T(8,128)}, f32[32,1024]{1,0:T(8,128)}) async-done(((f32[32,1024]{1,0:T(8,128)}, f32[32,1024]{1,0:T(8,128)}, f32[32,1024]{1,0:T(8,128)}), (f32[32,1024]{1,0:T(8,128)}, f32[32,1024]{1,0:T(8,128)}, f32[32,1024]{1,0:T(8,128)})) %all-reduce.30.cloned.1.call-update) | async-done | bytes 393232 | tf_op jit(solution)/shard_map/psum | solution.py:14
  106.3 3.0 %multiply_subtract_fusion.71 = (f32[2,1,32,1024]{3,2,1,0:T(8,128)S(1)}, f32[2,1,32,1024]{3,2,1,0:T(8,128)S(1)}, f32[2,1,32,1024]{3,2,1,0:T(8,128)S(1)}, f32[2,1,...) fusion(f32[2]{0:T(128)S(1)} %get-tuple-element.29, ...), kind=kLoop, calls=%fused_computation.386 | loop fusion | flops 1900544 | bytes 2621496 | tf_op jit(solution)/shard_map/sub | solution.py:40
  110.0 0.6 slice_add_fusion.8
  110.6 0.6 slice_add_fusion.10
  112.6 0.6 fusion.4
  113.9 0.7 fusion.12
  114.7 0.7 fusion.6
  116.1 0.7 fusion.14
  116.8 0.7 fusion.8
  118.3 0.8 copy-done.2
  119.1 1.5 multiply_subtract_fusion.47
  121.3 0.6 slice_add_fusion.4
  121.9 0.6 slice_add_fusion.6
  125.1 0.7 fusion.24
  125.9 0.7 fusion.18
  127.3 0.7 fusion.26
  128.1 0.7 fusion.20
  129.5 0.8 copy-done.1
  130.3 1.5 multiply_subtract_fusion.23
  132.1 0.6 slice_add_fusion
  133.0 0.6 slice_add_fusion.2
  136.4 0.7 fusion.36
  137.1 0.7 fusion.30
  138.5 0.7 fusion.38
  139.3 0.7 fusion.32
  140.9 0.8 pad_maximum_fusion
  143.6 88.7 %all-reduce.28.cloned.1.call-done = f32[3,32,1024]{2,1,0:T(8,128)} async-done(((f32[3,32,1024]{2,1,0:T(8,128)}), f32[3,32,1024]{2,1,0:T(8,128)}) %all-reduce.28.cloned.1.call-update) | async-done | bytes 393232 | tf_op jit(solution)/shard_map/psum | solution.py:115
  232.3 1.7 fusion.112
  (111 shorter events, 15.7 us)
Async XLA Ops:
  6.5 99.8 %all-reduce.30.cloned.1.call-start = ((), (), s32[]{:S(2)}) async-start(), calls=%async_computation.1 | async-start | bytes 786432 | tf_op jit(solution)/shard_map/psum | solution.py:14
  6.5 0.7 copy-start.3
  9.7 1.8 copy-start.5
  9.7 2.1 copy-start.6
  9.7 4.0 %copy-start.4 = (f32[2,2]{1,0:T(2,128)S(1)}, f32[2,2]{1,0:T(2,128)}, u32[]{:S(2)}) copy-start(f32[2,2]{1,0:T(2,128)} %param.7) | copy-start | bytes 52
  11.4 95.0 %copy-start = (f32[2,2,32,1024]{3,2,1,0:T(8,128)S(1)}, f32[2,2,32,1024]{3,2,1,0:T(8,128)}, u32[]{:S(2)}) copy-start(f32[2,2,32,1024]{3,2,1,0:T(8,128)} %param.6) | copy-start | bytes 1572868
  11.4 220.9 %all-reduce.28.cloned.1.call-start = ((), (), s32[]{:S(2)}) async-start(), calls=%async_computation | async-start | bytes 786432 | tf_op jit(solution)/shard_map/psum | solution.py:115
  118.2 0.9 copy-start.2
  129.4 0.9 copy-start.1
Sparse Core Ops, SparseCore 0:
  11.5 94.7 all-reduce.29
  141.9 90.3 all-reduce.27
where the time goes:
time: 241 us
  waiting for transfers between devices  180 us (75%)
  other arithmetic  36.8 us (15%)
  between operations  19.1 us (8%)
  local copies, waits for them, and re-layouts  4.73 us (2%)
    psum x1, waiting for transfers between devices, broadcast(): return lax.psum(kept, axis)  91.4 us
    psum x1, waiting for transfers between devices, local(): summed_stack = lax.psum(jnp.stack(partials), 'freq')  88.7 us
    add x24, other arithmetic, directional(): outer_pair = adjacent(2) + adjacent(-2)  15.3 us
    sub x36, other arithmetic, complex_mul(): values[:, 0] * coef_re - values[:, 1] * coef_im  12.8 us
  transfers between devices with their start and end apart: 2, of which 2 were waited for; matrix products, arithmetic and copies ran while one was open for 1% of the time, Pallas kernels for 0%

commit v1 on v0

--- a/solution.py
+++ b/solution.py
@@ -9,9 +9,15 @@
 directions = ((1, 0), (0, 1), (1, 1), (1, -1))
 
 
+def gather_and_add(array, mesh_axis):
+    blocks = lax.all_gather(array, mesh_axis, axis=0, tiled=False)
+    total = blocks.sum(axis=0)
+    return total
+
+
 def broadcast(value, axis, source):
     kept = jnp.where(lax.axis_index(axis) == source, value, 0).astype(value.dtype)
-    return lax.psum(kept, axis)
+    return gather_and_add(kept, axis)
 
 
 def source_start(spectrum, position, freq_index, freq_total, height, breadth):

time: 241 us -> 253 us (1.050)
  waiting for transfers between devices: 180 us -> 187 us
  other arithmetic: 36.8 us -> 41.1 us
    all_gather x0 -> x3, waiting for transfers between devices: none -> 96.9 us  [gather_and_add(): blocks = lax.all_gather(array, mesh_axis, axis=0, tiled=False)]
    psum x1 -> x0, waiting for transfers between devices: 91.4 us -> none  [broadcast(): return lax.psum(kept, axis)]
    reduce_sum x0 -> x3, other arithmetic: none -> 5.14 us  [gather_and_add(): total = blocks.sum(axis=0)]
  transfers between devices with their start and end apart: 2 -> 4, of which waited for: 2 -> 4; matrix products, arithmetic and copies ran while one was open for 1% -> 11% of each run, Pallas kernels for 0% -> 0%
where the time goes in v1:
time: 253 us; the launch traced here: 252 us
  waiting for transfers between devices  187 us (74%)
  other arithmetic  41.1 us (16%)
  between operations  18.7 us (7%)
  local copies, waits for them, and re-layouts  5.55 us (2%)
    all_gather x3, waiting for transfers between devices, gather_and_add(): blocks = lax.all_gather(array, mesh_axis, axis=0, tiled=False)  96.9 us
    psum x1, waiting for transfers between devices, local(): summed_stack = lax.psum(jnp.stack(partials), 'freq')  88.4 us
    add x24, other arithmetic, directional(): outer_pair = adjacent(2) + adjacent(-2)  15.3 us
    sub x36, other arithmetic, complex_mul(): values[:, 0] * coef_re - values[:, 1] * coef_im  12 us
    reduce_sum x3, other arithmetic, gather_and_add(): total = blocks.sum(axis=0)  5.14 us
  transfers between devices with their start and end apart: 4, of which 4 were waited for; matrix products, arithmetic and copies ran while one was open for 11% of the time, Pallas kernels for 0%

profile of v1, /device:TPU:0, one launch (start us, length us, event | category | flops | bytes accessed | tf_op | source)
XLA Modules:
  0.0 252.2 jit_solution(674821643487797101)
XLA Ops:
  6.5 1.4 fusion.131
  9.7 1.6 broadcast_select_fusion
  11.5 0.7 all-gather.6.cloned.1.call-update
  12.2 0.7 all-gather.8.cloned.1.call-update
  13.0 0.8 fusion.129
  14.1 1.3 fusion.130
  16.7 1.0 slice_reduce_fusion.25
  18.7 37.0 %all-gather.4.cloned.1.call-done = f32[16,32,1024]{2,1,0:T(8,128)} async-done(((f32[1,32,1024]{2,1,0:T(8,128)}), f32[16,32,1024]{2,1,0:T(8,128)}) %all-gather.4.cloned.1.call-update) | async-done | bytes 2097168 | tf_op jit(solution)/shard_map/all_gather | solution.py:13
  55.8 1.7 reduce_sum.54
  57.5 2.1 multiply_subtract_fusion.71
  60.9 0.6 slice_add_fusion.10
  64.1 0.7 fusion.12
  64.9 0.7 fusion.6
  66.3 0.7 fusion.14
  67.1 0.7 fusion.8
  68.5 29.6 %all-gather.6.cloned.1.call-done = f32[16,32,1024]{2,1,0:T(8,128)} async-done(((f32[1,32,1024]{2,1,0:T(8,128)}), f32[16,32,1024]{2,1,0:T(8,128)}) %all-gather.6.cloned.1.call-update) | async-done | bytes 2097168 | tf_op jit(solution)/shard_map/all_gather | solution.py:13
  98.1 1.7 reduce_sum.56
  99.8 1.5 multiply_subtract_fusion.47
  105.9 0.7 fusion.24
  106.6 0.7 fusion.18
  108.1 0.7 fusion.26
  108.8 0.7 fusion.20
  110.3 30.3 %all-gather.8.cloned.1.call-done = f32[16,32,1024]{2,1,0:T(8,128)} async-done(((f32[1,32,1024]{2,1,0:T(8,128)}), f32[16,32,1024]{2,1,0:T(8,128)}) %all-gather.8.cloned.1.call-update) | async-done | bytes 2097168 | tf_op jit(solution)/shard_map/all_gather | solution.py:13
  140.6 1.7 reduce_sum.58
  142.3 1.5 multiply_subtract_fusion.23
  148.3 0.7 fusion.36
  149.1 0.7 fusion.30
  150.5 0.7 fusion.38
  151.3 0.7 fusion.32
  152.9 0.8 pad_maximum_fusion
  155.5 88.4 %all-reduce.26.cloned.1.call-done = f32[3,32,1024]{2,1,0:T(8,128)} async-done(((f32[3,32,1024]{2,1,0:T(8,128)}), f32[3,32,1024]{2,1,0:T(8,128)}) %all-reduce.26.cloned.1.call-update) | async-done | bytes 393232 | tf_op jit(solution)/shard_map/psum | solution.py:121
  243.9 1.7 fusion.112
  (108 shorter events, 19.3 us)
Async XLA Ops:
  6.5 50.9 %copy-start = (f32[2,2,32,1024]{3,2,1,0:T(8,128)S(1)}, f32[2,2,32,1024]{3,2,1,0:T(8,128)}, u32[]{:S(2)}) copy-start(f32[2,2,32,1024]{3,2,1,0:T(8,128)} %param.6) | copy-start | bytes 1572868
  6.5 49.2 %all-gather.4.cloned.1.call-start = ((), (), s32[]{:S(2)}) async-start(), calls=%async_computation | async-start | bytes 2228224 | tf_op jit(solution)/shard_map/all_gather | solution.py:13
  11.4 86.7 %all-gather.6.cloned.1.call-start = ((), (), s32[]{:S(2)}) async-start(), calls=%async_computation.1 | async-start | bytes 2228224 | tf_op jit(solution)/shard_map/all_gather | solution.py:13
  12.2 128.4 %all-gather.8.cloned.1.call-start = ((), (), s32[]{:S(2)}) async-start(), calls=%async_computation.2 | async-start | bytes 2228224 | tf_op jit(solution)/shard_map/all_gather | solution.py:13
  12.9 231.0 %all-reduce.26.cloned.1.call-start = ((), (), s32[]{:S(2)}) async-start(), calls=%async_computation.3 | async-start | bytes 786432 | tf_op jit(solution)/shard_map/psum | solution.py:121
Sparse Core Ops, SparseCore 0:
  11.5 44.1 all-gather.3
  57.9 40.1 all-gather.5
  100.3 40.2 all-gather.7
  153.8 90.0 all-reduce.25
